TPU v7x, 32 devices: a whole 2x2x4 slice. The times are simulated.
32 devices in a mesh: row: 16 (over z, x, core), col: 2 (over y).
Axes of the slice: x: 2, y: 2, z: 4, core: 2. Of those that a mesh axis runs over, the one named last changes fastest.
Arguments:
- template: float32 [32, 16, 2048], P(None, 'row', 'col'), may hold values from -6 to 6
- target: float32 [32, 16, 2048], P(None, 'row', 'col'), may hold values from -6 to 6
- velocity: float32 [3, 32, 16, 2048], P(None, None, 'row', 'col'), may hold values from -0.6 to 0.6
- departure: int32 [32, 1, 2048], P('row', None, 'col'), may hold values from -48 to 48
- weights: float32 [8, 4], replicated, may hold values from -0.1 to 1, as said below
Outputs:
- gradient: float32 [3, 32, 16, 2048], P(None, 'row', 'col')
Inputs may be any that keep to these rules, and one draw needn't show every extreme that they name: Row q holds the four weights of a cubic interpolation at a fraction between q / 8 and (q + 1) / 8; each row sums to one.
All inputs are finite; a program needn't handle non-finite values.
Results may differ from a plain program's by a relative error of at most 0.0001.
Values sent between devices are 32-bit elements; how exact they have to be, the bound alone decides.
A program may use at most 64 MiB of HBM per device.

v0:
```python
import math

import jax
import jax.numpy as jnp
from jax import lax
from jax.sharding import PartitionSpec as P

QUANT = 8
TAPS = 4


BETA = 0.5
HIGH = lax.Precision.HIGHEST


def with_halo(block, sides, width):
    for axis, dim in sides:
        count = lax.axis_size(axis)
        forward = [(i, i + 1) for i in range(count - 1)]
        forward.append((count - 1, 0))
        backward = [(target, source) for source, target in forward]
        low = lax.ppermute(
            lax.slice_in_dim(block, block.shape[dim] - width, None, axis=dim), axis, forward
        )
        high = lax.ppermute(lax.slice_in_dim(block, 0, width, axis=dim), axis, backward)
        block = jnp.concatenate([low, block, high], axis=dim)
    return block


def central(values, axis):
    return (jnp.roll(values, -1, axis) - jnp.roll(values, 1, axis)) * 0.5


def second_difference(values, axis):
    return 2.0 * values - jnp.roll(values, -1, axis) - jnp.roll(values, 1, axis)


def transport(template_y, departure, weights):
    planes, lines, columns = template_y.shape
    blocks = departure.shape[1]
    span = lines // blocks
    shift_cells = jnp.floor_divide(departure, QUANT)
    levels = departure - shift_cells * QUANT
    expanded = jnp.broadcast_to(
        shift_cells[:, :, None, :], (planes, blocks, span, columns)
    ).reshape(planes, lines, columns)
    chosen = levels[..., None] == jnp.arange(QUANT, dtype=jnp.int32)
    line_index = jnp.arange(lines, dtype=jnp.int32)[None, :, None]
    moved_image = jnp.zeros(template_y.shape, jnp.float32)
    for tap in range(TAPS):
        tap_weight = jnp.sum(jnp.where(chosen, weights[:, tap], 0.0), axis=-1)
        tap_weight = jnp.broadcast_to(
            tap_weight[:, :, None, :], (planes, blocks, span, columns)
        ).reshape(planes, lines, columns)
        source_index = jnp.mod(line_index - expanded - 1 + tap, lines)
        moved_image = moved_image + tap_weight * jnp.take_along_axis(
            template_y, source_index, axis=1
        )
    return moved_image


def curvature(velocity_z):
    field_shape = velocity_z.shape
    length = field_shape[-1]
    inner = 128
    outer = length // inner
    lines = velocity_z.reshape(-1, outer, inner)
    angle = 2.0 * math.pi / length
    outer_index = jnp.arange(outer, dtype=jnp.int32)
    inner_index = jnp.arange(inner, dtype=jnp.int32)
    outer_phase = (
        jnp.mod(outer_index[:, None] * outer_index[None, :] * inner, length).astype(jnp.float32)
        * angle
    )
    cos_outer = jnp.cos(outer_phase)
    sin_outer = jnp.sin(outer_phase)
    twist_phase = (
        jnp.mod(outer_index[:, None] * inner_index[None, :], length).astype(jnp.float32) * angle
    )
    cos_twist = jnp.cos(twist_phase)
    sin_twist = jnp.sin(twist_phase)
    inner_phase = (
        jnp.mod(inner_index[:, None] * inner_index[None, :] * outer, length).astype(jnp.float32)
        * angle
    )
    cos_inner = jnp.cos(inner_phase)
    sin_inner = jnp.sin(inner_phase)
    freq_index = outer_index[:, None] + outer * inner_index[None, :]
    signed = jnp.where(freq_index < length // 2, freq_index, freq_index - length).astype(
        jnp.float32
    )
    symbol = (signed * angle) ** 2 / length
    real_one = jnp.einsum("lap,ak->lkp", lines, cos_outer, precision=HIGH)
    imag_one = -jnp.einsum("lap,ak->lkp", lines, sin_outer, precision=HIGH)
    real_two = real_one * cos_twist + imag_one * sin_twist
    imag_two = imag_one * cos_twist - real_one * sin_twist
    real_three = jnp.einsum("lkp,pq->lkq", real_two, cos_inner, precision=HIGH) + jnp.einsum(
        "lkp,pq->lkq", imag_two, sin_inner, precision=HIGH
    )
    imag_three = jnp.einsum("lkp,pq->lkq", imag_two, cos_inner, precision=HIGH) - jnp.einsum(
        "lkp,pq->lkq", real_two, sin_inner, precision=HIGH
    )
    real_three = real_three * symbol
    imag_three = imag_three * symbol
    real_four = jnp.einsum("lkq,pq->lkp", real_three, cos_inner, precision=HIGH) - jnp.einsum(
        "lkq,pq->lkp", imag_three, sin_inner, precision=HIGH
    )
    imag_four = jnp.einsum("lkq,pq->lkp", imag_three, cos_inner, precision=HIGH) + jnp.einsum(
        "lkq,pq->lkp", real_three, sin_inner, precision=HIGH
    )
    real_five = real_four * cos_twist - imag_four * sin_twist
    imag_five = imag_four * cos_twist + real_four * sin_twist
    result = jnp.einsum("lkp,kn->lnp", real_five, cos_outer, precision=HIGH) - jnp.einsum(
        "lkp,kn->lnp", imag_five, sin_outer, precision=HIGH
    )
    return result.reshape(field_shape)


def spectral(arrived):
    return (arrived, curvature(arrived[3:6]))


def per_device(template, target, velocity, departure, weights):
    across = second_difference(velocity, 1)
    bundle = jnp.concatenate([template[None], target[None], velocity, across], axis=0)
    regrouped = lax.all_to_all(bundle, "row", split_axis=1, concat_axis=2, tiled=True)
    moved_image = transport(regrouped[0], departure, weights)
    misfit = regrouped[1] - moved_image
    pull_along = misfit * central(moved_image, 1)
    velocity_y = regrouped[2:5]
    second_part = second_difference(velocity_y, 2)
    second_part = regrouped[5:8] + second_part
    outgoing = jnp.concatenate(
        [misfit[None], moved_image[None], pull_along[None], velocity_y, second_part], axis=0
    )
    columns_z, bending = spectral(
        lax.all_to_all(outgoing, "col", split_axis=2, concat_axis=3, tiled=True)
    )
    misfit_z = columns_z[0]
    moved_z = columns_z[1]
    second_z = columns_z[6:9]
    padded = with_halo(moved_z, (("row", 0),), 1)
    slope_across = (padded[2:] - padded[:-2]) * 0.5
    force = jnp.stack([misfit_z * slope_across, columns_z[2], misfit_z * central(moved_z, 2)])
    return BETA * (second_z + bending) + force


def solution(mesh):
    in_specs = (
        P(None, "row", "col"),
        P(None, "row", "col"),
        P(None, None, "row", "col"),
        P("row", None, "col"),
        P(),
    )
    out_specs = P(None, "row", "col", None)
    return jax.shard_map(
        per_device, mesh=mesh, in_specs=in_specs, out_specs=out_specs, check_vma=False
    )
```

profile of v0, /device:TPU:0, one launch (start us, length us, event | category | flops | bytes accessed | tf_op | source)
XLA Modules:
  0.0 1363.4 jit_solution(3733169754622436513)
XLA Ops:
  0.0 1.7 fusion.183
  1.8 1.1 fusion.5
  2.9 1.9 pad_maximum_fusion
  4.8 7.5 all-to-all-start
  13.1 0.7 select_reduce_fusion.3
  13.8 21.4 %all-to-all-done = f32[8,32,1,1024]{3,2,0,1:T(1,128)S(1)} async-done(((f32[8,32,1,1024]{3,2,0,1:T(1,128)}), f32[8,32,1,1024]{3,2,0,1:T(1,128)S(1)}, u32[]{:S(2)}, u32[]{:S(2)}) %all-to-all-start) | async-done | bytes 1048608 | tf_op jit(solution)/shard_map/all_to_all | solution.py:126
  36.1 1.0 copy-done
  37.1 320.9 %gather_fusion.1 = f32[32768]{0:T(1024)S(1)} fusion(f32[2,16,1024]{2,1,0:T(8,128)S(1)} %slice_bitcast_fusion.4, s32[32768]{0:T(1024)S(1)} %bitcast.168), kind=kCustom, calls=%fused_computation.1.clone | custom fusion | bytes 655360 | tf_op jit(solution)/shard_map/jit(take_along_axis)/gather | solution.py:56
  358.1 320.9 %gather_fusion.2 = f32[32768]{0:T(1024)S(1)} fusion(f32[2,16,1024]{2,1,0:T(8,128)S(1)} %slice_bitcast_fusion.4, s32[32768]{0:T(1024)S(1)} %bitcast.167), kind=kCustom, calls=%fused_computation.2.clone | custom fusion | bytes 655360 | tf_op jit(solution)/shard_map/jit(take_along_axis)/gather | solution.py:56
  679.1 320.9 %gather_fusion.3 = f32[32768]{0:T(1024)S(1)} fusion(f32[2,16,1024]{2,1,0:T(8,128)S(1)} %slice_bitcast_fusion.4, s32[32768]{0:T(1024)S(1)} %bitcast.166), kind=kCustom, calls=%fused_computation.3.clone | custom fusion | bytes 655360 | tf_op jit(solution)/shard_map/jit(take_along_axis)/gather | solution.py:56
  1000.1 320.9 %gather_fusion = f32[32768]{0:T(1024)S(1)} fusion(f32[2,16,1024]{2,1,0:T(8,128)S(1)} %slice_bitcast_fusion.4, s32[32768]{0:T(1024)S(1)} %bitcast.165), kind=kCustom, calls=%fused_computation.clone | custom fusion | bytes 655360 | tf_op jit(solution)/shard_map/jit(take_along_axis)/gather | solution.py:56
  1322.0 2.0 copy.107
  1323.9 3.8 all-to-all-start.1
  1327.8 15.9 %all-to-all-done.1 = f32[9,2,16,1024]{3,1,0,2:T(2,128)S(1)} async-done(((f32[9,2,16,1024]{3,1,0,2:T(2,128)}), f32[9,2,16,1024]{3,1,0,2:T(2,128)S(1)}, u32[]{:S(2)}, u32[]{:S(2)}) %all-to-all-start.1) | async-done | bytes 1179680 | tf_op jit(solution)/shard_map/all_to_all | solution.py:137
  1345.8 0.7 fusion.11
  1346.5 0.7 fusion.7
  1347.5 0.7 fusion.1
  1348.2 0.7 fusion.57
  1348.9 0.7 fusion.2
  1350.4 0.7 convolution_subtract_fusion.1
  1351.1 0.7 convolution_add_fusion
  1351.9 4.3 collective-permute-start
  1358.1 4.5 collective-permute-done.1
  1362.6 0.8 maximum_add_fusion
  (73 shorter events, 7.4 us)
Async XLA Ops:
  0.0 1.7 copy-start.2
  1.8 1.2 copy-start.5
  1.8 1.2 copy-start.6
  4.8 7.5 copy-start.11
  4.8 30.4 %all-to-all-start = ((f32[8,32,1,1024]{3,2,0,1:T(1,128)}), f32[8,32,1,1024]{3,2,0,1:T(1,128)S(1)}, u32[]{:S(2)}, u32[]{:S(2)}) async-start(f32[8,32,1,1024]{3,2,0,1:T(1,128)} %pad_maximum_fusion), calls=%async_computation | async-start | bytes 2097152 | tf_op jit(solution)/shard_map/all_to_all | solution.py:126
  12.4 0.7 copy-start.12
  12.5 0.6 copy-start.3
  36.1 1.0 copy-start
  1000.0 321.0 %copy-start.1 = (f32[8,16,2,1,1024]{4,1,2,3,0:T(8,128)S(1)}, f32[8,16,2,1,1024]{4,1,2,3,0:T(8,128)}, u32[]{:S(2)}) copy-start(f32[8,16,2,1,1024]{4,1,2,3,0:T(8,128)} %copy-done) | copy-start | bytes 3145732
  1000.0 321.0 %copy-start.4 = (s32[2,1024]{1,0:T(2,128)S(1)}, s32[2,1024]{1,0:T(2,128)}, u32[]{:S(2)}) copy-start(s32[2,1024]{1,0:T(2,128)} %copy-done.3) | copy-start | bytes 24580
  1000.0 321.0 %copy-start.7 = (f32[2,1024]{1,0:T(2,128)S(1)}, f32[2,1024]{1,0:T(2,128)}, u32[]{:S(2)}) copy-start(f32[2,1024]{1,0:T(2,128)} %get-tuple-element.6) | copy-start | bytes 24580
  1000.1 321.0 %copy-start.8 = (f32[2,1024]{1,0:T(2,128)S(1)}, f32[2,1024]{1,0:T(2,128)}, u32[]{:S(2)}) copy-start(f32[2,1024]{1,0:T(2,128)} %get-tuple-element.7) | copy-start | bytes 24580
  1000.1 321.0 %copy-start.9 = (f32[2,1024]{1,0:T(2,128)S(1)}, f32[2,1024]{1,0:T(2,128)}, u32[]{:S(2)}) copy-start(f32[2,1024]{1,0:T(2,128)} %get-tuple-element.8) | copy-start | bytes 24580
  1000.1 321.0 %copy-start.10 = (f32[2,1024]{1,0:T(2,128)S(1)}, f32[2,1024]{1,0:T(2,128)}, u32[]{:S(2)}) copy-start(f32[2,1024]{1,0:T(2,128)} %get-tuple-element.9) | copy-start | bytes 24580
  1323.9 19.7 %all-to-all-start.1 = ((f32[9,2,16,1024]{3,1,0,2:T(2,128)}), f32[9,2,16,1024]{3,1,0,2:T(2,128)S(1)}, u32[]{:S(2)}, u32[]{:S(2)}) async-start(f32[9,2,16,1024]{3,1,0,2:T(2,128)} %copy.107), calls=%async_computation.1 | async-start | bytes 2359296 | tf_op jit(solution)/shard_map/all_to_all | solution.py:137
  1351.9 6.2 collective-permute-start
  1356.2 6.4 collective-permute-start.1
where the time goes:
time: 1360 us
  local copies, waits for them, and re-layouts  1290 us (95%)
  waiting for transfers between devices  42.4 us (3%)
  starting transfers between devices  15.6 us (1%)
    gather x8, local copies, waits for them, and re-layouts, transport(): jnp.take_along_axis(template_y, source_index, axis=1)  1280 us
  transfers between devices with their start and end apart: 4, of which 4 were waited for; matrix products, arithmetic and copies ran while one was open for 0% of the time, Pallas kernels for 0%

commit v1 on v0

--- a/solution.py
+++ b/solution.py
@@ -1,8 +1,12 @@
+import functools
 import math
 
 import jax
 import jax.numpy as jnp
+import numpy as np
 from jax import lax
+from jax.experimental import pallas as pl
+from jax.experimental.pallas import tpu as pltpu
 from jax.sharding import PartitionSpec as P
 
 QUANT = 8
@@ -11,6 +15,9 @@
 
 BETA = 0.5
 HIGH = lax.Precision.HIGHEST
+LANES = 128
+SUBLANES = 8
+MESH = pl.DeviceIdType.MESH
 
 
 def with_halo(block, sides, width):
@@ -35,28 +42,38 @@
     return 2.0 * values - jnp.roll(values, -1, axis) - jnp.roll(values, 1, axis)
 
 
+def tap_weights(levels, weight):
+    taps = []
+    for tap in range(TAPS):
+        value = jnp.zeros(levels.shape, jnp.float32)
+        for level in range(QUANT):
+            value = jnp.where(levels == level, weight(level, tap), value)
+        taps.append(value)
+    return taps
+
+
 def transport(template_y, departure, weights):
     planes, lines, columns = template_y.shape
     blocks = departure.shape[1]
     span = lines // blocks
     shift_cells = jnp.floor_divide(departure, QUANT)
     levels = departure - shift_cells * QUANT
-    expanded = jnp.broadcast_to(
-        shift_cells[:, :, None, :], (planes, blocks, span, columns)
-    ).reshape(planes, lines, columns)
-    chosen = levels[..., None] == jnp.arange(QUANT, dtype=jnp.int32)
-    line_index = jnp.arange(lines, dtype=jnp.int32)[None, :, None]
-    moved_image = jnp.zeros(template_y.shape, jnp.float32)
-    for tap in range(TAPS):
-        tap_weight = jnp.sum(jnp.where(chosen, weights[:, tap], 0.0), axis=-1)
-        tap_weight = jnp.broadcast_to(
-            tap_weight[:, :, None, :], (planes, blocks, span, columns)
-        ).reshape(planes, lines, columns)
-        source_index = jnp.mod(line_index - expanded - 1 + tap, lines)
-        moved_image = moved_image + tap_weight * jnp.take_along_axis(
-            template_y, source_index, axis=1
-        )
-    return moved_image
+    taps = tap_weights(levels, lambda level, tap: weights[level, tap])
+    shift = jnp.mod(shift_cells + 1, lines)
+    parts = []
+    for block in range(blocks):
+        rolled = template_y
+        step = 1
+        while step < lines:
+            chosen = (shift[:, block : block + 1] & step) != 0
+            rolled = jnp.where(chosen, jnp.roll(rolled, step, 1), rolled)
+            step *= 2
+        part = 0.0
+        for tap in range(TAPS):
+            turned = jnp.roll(rolled, -tap - block * span, 1)[:, :span]
+            part = part + taps[tap][:, block : block + 1] * turned
+        parts.append(part)
+    return jnp.concatenate(parts, axis=1)
 
 
 def curvature(velocity_z):
@@ -145,6 +162,439 @@
     return BETA * (second_z + bending) + force
 
 
+def split_halves(values):
+    high = values.astype(jnp.bfloat16)
+    return high, (values - high.astype(jnp.float32)).astype(jnp.bfloat16)
+
+
+def dot_split(left, right):
+    dot = functools.partial(jnp.dot, preferred_element_type=jnp.float32)
+    return dot(left[0], right[0]) + (dot(left[0], right[1]) + dot(left[1], right[0]))
+
+
+def halves_of(matrix):
+    high = matrix.astype(np.float32).astype(jnp.bfloat16)
+    low = (matrix - high.astype(np.float64)).astype(np.float32).astype(jnp.bfloat16)
+    return np.stack([high, low])
+
+
+def operators(length, rows):
+    outer = length // LANES
+    frequency = np.fft.fftfreq(length) * length
+    response = np.real(np.fft.ifft((2.0 * math.pi / length * frequency) ** 2))
+    response[0] += 4.0
+    response *= BETA
+    inner = np.arange(LANES)
+    group = np.arange(outer)
+    away = np.mod(
+        LANES * group[:, None, None] + inner[None, :, None] - inner[None, None, :], length
+    )
+    mixed = np.fft.fft(response[away], axis=0)
+    pairs = []
+    forward = np.zeros((outer, outer))
+    inverse = np.zeros((outer, outer))
+    forward[0] = 1.0
+    forward[1] = (-1.0) ** group
+    inverse[:, 0] = 1.0 / outer
+    inverse[:, 1] = (-1.0) ** group / outer
+    zero = np.zeros((LANES, LANES))
+    pairs.append(np.block([[mixed[0].real.T, zero], [zero, mixed[outer // 2].real.T]]))
+    for k in range(1, outer // 2):
+        real, imag = mixed[k].real.T, mixed[k].imag.T
+        pairs.append(np.block([[real, imag], [-imag, real]]))
+        phase = 2.0 * math.pi * k * group / outer
+        forward[2 * k] = np.cos(phase)
+        forward[2 * k + 1] = -np.sin(phase)
+        inverse[:, 2 * k] = 2.0 * np.cos(phase) / outer
+        inverse[:, 2 * k + 1] = -2.0 * np.sin(phase) / outer
+    same = np.eye(rows)
+    ahead = np.einsum("ka,yz->kyza", forward, same).reshape(outer * rows, rows * outer)
+    back = np.einsum("ak,yz->yakz", inverse, same).reshape(rows * outer, outer * rows)
+    return halves_of(ahead), halves_of(np.stack(pairs)), halves_of(back)
+
+
+def kernel(
+    extent,
+    template,
+    target,
+    velocity,
+    departure,
+    weights,
+    ahead_hbm,
+    pairs_hbm,
+    back_hbm,
+    out,
+    template_y,
+    target_z,
+    velocity_z,
+    extended,
+    moved,
+    moved_low,
+    moved_high,
+    velocity_low,
+    velocity_high,
+    spectrum,
+    ahead,
+    pairs,
+    back,
+    load_sem,
+    send_sem,
+    recv_sem,
+):
+    rows, columns = extent
+    row, column = lax.axis_index("row"), lax.axis_index("col")
+    planes, lines, slab = template_y.shape[:3]
+    components = velocity_z.shape[0]
+    own = lines // columns
+    outer = columns * slab
+    owner = row // own
+    place = lax.rem(row, own)
+    TEMPLATE, TARGET, MOVED, LOW, HIGH_SIDE, VELOCITY = 0, 1, 2, 3, 4, 5
+    VLOW, VHIGH = VELOCITY + components, VELOCITY + 2 * components
+
+    loads = [
+        pltpu.make_async_copy(source, sink, load_sem.at[i])
+        for i, (source, sink) in enumerate(
+            [(ahead_hbm, ahead), (pairs_hbm, pairs), (back_hbm, back)]
+        )
+    ]
+    for load in loads:
+        load.start()
+
+    barrier = pltpu.get_barrier_semaphore()
+    for i in range(rows):
+        for j in range(columns):
+            if i + j > 0:
+                pl.semaphore_signal(
+                    barrier,
+                    inc=1,
+                    device_id=(lax.rem(row + i, rows), lax.rem(column + j, columns)),
+                    device_id_type=MESH,
+                )
+    pl.semaphore_wait(barrier, rows * columns - 1)
+
+    def remote(source, sink, kind, to):
+        return pltpu.make_async_remote_copy(
+            src_ref=source,
+            dst_ref=sink,
+            send_sem=send_sem.at[kind],
+            recv_sem=recv_sem.at[kind],
+            device_id=to,
+            device_id_type=MESH,
+        )
+
+    pending = []
+
+    def deliver(source, sink, kind, to, near):
+        if near is None:
+            remote(source, sink, kind, to).start()
+            pending.append((None, source, sink, kind, to))
+            return
+
+        @pl.when(near == column)
+        def _():
+            pltpu.make_async_copy(source, sink, recv_sem.at[kind]).start()
+
+        @pl.when(near != column)
+        def _():
+            remote(source, sink, kind, to).start()
+
+        pending.append((near, source, sink, kind, to))
+
+    def exchange(order):
+        return [(i, lax.rem(row + i, rows)) for i in order]
+
+    def arrived(ref, kind):
+        pltpu.make_async_copy(ref, ref, recv_sem.at[kind]).wait()
+
+    order = list(range(1, rows)) + [0]
+    for i, to in exchange(order):
+        source = template.at[pl.ds(to * planes, planes)]
+        sink = template_y.at[:, row]
+        if i == 0:
+            pltpu.make_async_copy(source, sink, recv_sem.at[TEMPLATE]).start()
+        else:
+            deliver(source, sink, TEMPLATE, (to, column), None)
+    for i, to in exchange(order):
+        deliver(
+            target.at[pl.ds(to * planes, planes)],
+            target_z.at[:, place, column],
+            TARGET,
+            (to, owner),
+            owner if i == 0 else None,
+        )
+    before = lax.rem(owner + columns - 1, columns)
+    after = lax.rem(owner + 1, columns)
+
+    def send_velocity(comp):
+        for i, to in exchange(order):
+            source = velocity.at[comp, pl.ds(to * planes, planes)]
+            deliver(
+                source,
+                velocity_z.at[comp, :, place + 1, column],
+                VELOCITY + comp,
+                (to, owner),
+                owner if i == 0 else None,
+            )
+
+    def edges(act):
+        @pl.when(place == 0)
+        def _():
+            for comp in range(components):
+                for i, to in exchange(order):
+                    act(comp, i, to, own + 1, before)
+
+        @pl.when(place == own - 1)
+        def _():
+            for comp in range(components):
+                for i, to in exchange(order):
+                    act(comp, i, to, 0, after)
+
+    def edge_copy(comp, to, line, where):
+        return (
+            velocity.at[comp, pl.ds(to * planes, planes)],
+            velocity_z.at[comp, :, line, column],
+            VELOCITY + comp,
+            (to, where),
+        )
+
+    def start_edge(comp, i, to, line, where):
+        copy = edge_copy(comp, to, line, where)
+        if i > 0:
+            remote(*copy).start()
+            return
+
+        @pl.when(where == column)
+        def _():
+            pltpu.make_async_copy(copy[0], copy[1], recv_sem.at[copy[2]]).start()
+
+        @pl.when(where != column)
+        def _():
+            remote(*copy).start()
+
+    def wait_edge(comp, i, to, line, where):
+        copy = edge_copy(comp, to, line, where)
+        if i > 0:
+            remote(*copy).wait_send()
+            return
+
+        @pl.when(where != column)
+        def _():
+            remote(*copy).wait_send()
+
+    edges(start_edge)
+    for comp in range(components):
+        send_velocity(comp)
+
+    arrived(template_y, TEMPLATE)
+    blocks = departure.shape[1]
+    span = lines // blocks
+    for plane in range(planes):
+        image = [template_y[plane, y] for y in range(lines)]
+        for block in range(blocks):
+            offset = departure[plane, block]
+            whole = offset >> (QUANT.bit_length() - 1)
+            levels = offset - whole * QUANT
+            taps = tap_weights(levels, lambda level, tap: weights[level, tap])
+            shift = jnp.where(whole + 1 < 0, whole + 1 + lines, whole + 1)
+            rolled = image
+            step = 1
+            while step < lines:
+                chosen = (shift & step) != 0
+                rolled = [
+                    jnp.where(chosen, rolled[(y - step) % lines], rolled[y]) for y in range(lines)
+                ]
+                step *= 2
+            for y in range(block * span, (block + 1) * span):
+                value = taps[0] * rolled[y]
+                for tap in range(1, TAPS):
+                    value = value + taps[tap] * rolled[(y + tap) % lines]
+                extended[plane, y + 1] = value
+                if y == lines - 1:
+                    extended[plane, 0] = value
+                if y == 0:
+                    extended[plane, lines + 1] = value
+    up, down = lax.rem(row + 1, rows), lax.rem(row + rows - 1, rows)
+    for j in range(1, columns):
+        to = lax.rem(column + j, columns)
+        deliver(
+            extended.at[:, pl.ds(to * own, own + 2)],
+            moved.at[column],
+            MOVED,
+            (row, to),
+            None,
+        )
+    for j in range(columns):
+        to = lax.rem(column + j, columns)
+        lines_of = pl.ds(to * own + 1, own)
+        deliver(
+            extended.at[planes - 1, lines_of], moved_low.at[:, column], LOW, (up, to), None
+        )
+        deliver(extended.at[0, lines_of], moved_high.at[:, column], HIGH_SIDE, (down, to), None)
+    moved[column] = extended[:, pl.ds(column * own, own + 2)]
+    for load in loads:
+        load.wait()
+
+    def whole_lines(values):
+        return values.reshape(values.shape[:-3] + (outer, LANES))
+
+    ahead_parts = (ahead[0], ahead[1])
+    back_parts = (back[0], back[1])
+    for comp in range(components):
+        arrived(velocity_z.at[comp], VELOCITY + comp)
+        deliver(
+            velocity_z.at[comp, planes - 1, pl.ds(1, own)],
+            velocity_low.at[comp],
+            VLOW + comp,
+            (up, column),
+            None,
+        )
+        deliver(
+            velocity_z.at[comp, 0, pl.ds(1, own)],
+            velocity_high.at[comp],
+            VHIGH + comp,
+            (down, column),
+            None,
+        )
+        for plane in range(planes):
+            block = velocity_z[comp, plane, 1 : own + 1].reshape(own * outer, LANES)
+            spectrum[:, comp, plane] = dot_split(ahead_parts, split_halves(block)).reshape(
+                outer, own, LANES
+            )
+        if comp > 0:
+            continue
+        arrived(target_z, TARGET)
+        for _ in range(columns - 1):
+            pltpu.make_async_copy(moved.at[0], moved.at[0], recv_sem.at[MOVED]).wait()
+        arrived(moved_low, LOW)
+        arrived(moved_high, HIGH_SIDE)
+        lane = lax.broadcasted_iota(jnp.int32, (own, outer, LANES), 2)
+        for plane in range(planes):
+            with_ends = jnp.concatenate(
+                [moved[j, plane] for j in range(columns)], axis=1
+            )
+            here = with_ends[1 : own + 1]
+            misfit = whole_lines(target_z[plane]) - here
+            half = 0.5 * misfit
+
+            def at(index):
+                if index < 0:
+                    return whole_lines(moved_low[...])
+                if index == planes:
+                    return whole_lines(moved_high[...])
+                return jnp.concatenate(
+                    [moved[j, index, 1 : own + 1] for j in range(columns)], axis=1
+                )
+
+            out[0, plane] = half * (at(plane + 1) - at(plane - 1))
+            out[1, plane] = half * (with_ends[2:] - with_ends[:-2])
+            following = jnp.roll(here, -1, 2)
+            following = jnp.where(lane == LANES - 1, jnp.roll(following, -1, 1), following)
+            previous = jnp.roll(here, 1, 2)
+            previous = jnp.where(lane == 0, jnp.roll(previous, 1, 1), previous)
+            out[2, plane] = half * (following - previous)
+
+    for pair in range(outer // 2):
+        shape = (components * planes * own, LANES)
+        joined = jnp.concatenate(
+            [spectrum[2 * pair].reshape(shape), spectrum[2 * pair + 1].reshape(shape)], axis=1
+        )
+        result = dot_split(split_halves(joined), (pairs[0, pair], pairs[1, pair]))
+        shape = (components, planes, own, LANES)
+        spectrum[2 * pair] = result[:, :LANES].reshape(shape)
+        spectrum[2 * pair + 1] = result[:, LANES:].reshape(shape)
+
+    for comp in range(components):
+        arrived(velocity_low.at[comp], VLOW + comp)
+        arrived(velocity_high.at[comp], VHIGH + comp)
+        for plane in range(planes):
+            block = spectrum[:, comp, plane].reshape(outer * own, LANES)
+            smooth = dot_split(back_parts, split_halves(block)).reshape(own, outer, LANES)
+            low = velocity_low[comp] if plane == 0 else velocity_z[comp, plane - 1, 1 : own + 1]
+            high = (
+                velocity_high[comp]
+                if plane == planes - 1
+                else velocity_z[comp, plane + 1, 1 : own + 1]
+            )
+            sides = whole_lines(
+                (low + high) + (velocity_z[comp, plane, :own] + velocity_z[comp, plane, 2:])
+            )
+            out[comp, plane] = out[comp, plane] + (smooth - BETA * sides)
+
+    for near, source, sink, kind, to in pending:
+        if near is None:
+            remote(source, sink, kind, to).wait_send()
+        else:
+
+            @pl.when(near != column)
+            def _():
+                remote(source, sink, kind, to).wait_send()
+
+    edges(wait_edge)
+
+
+def direct(template, target, velocity, departure, weights):
+    rows, columns = lax.axis_size("row"), lax.axis_size("col")
+    extent_x, _, cells = template.shape
+    components = velocity.shape[0]
+    planes = extent_x // rows
+    lines = rows
+    own = lines // columns
+    slab = cells // LANES
+    outer = slab * columns
+    ahead, pairs, back = operators(cells * columns, own)
+    tile = (slab, LANES)
+    hbm = pl.BlockSpec(memory_space=pl.ANY)
+    vmem = pl.BlockSpec(memory_space=pltpu.VMEM)
+    smem = pl.BlockSpec(memory_space=pltpu.SMEM)
+    kinds = 5 + 3 * components
+    result = pl.pallas_call(
+        functools.partial(kernel, (rows, columns)),
+        out_shape=jax.ShapeDtypeStruct((components, planes, own, outer, LANES), jnp.float32),
+        in_specs=[hbm, hbm, hbm, vmem, smem, hbm, hbm, hbm],
+        out_specs=vmem,
+        scratch_shapes=[
+            pltpu.VMEM((planes, lines) + tile, jnp.float32),
+            pltpu.VMEM((planes, own, columns) + tile, jnp.float32),
+            pltpu.VMEM((components, planes, own + 2, columns) + tile, jnp.float32),
+            pltpu.VMEM((planes, lines + 2) + tile, jnp.float32),
+            pltpu.VMEM((columns, planes, own + 2) + tile, jnp.float32),
+            pltpu.VMEM((own, columns) + tile, jnp.float32),
+            pltpu.VMEM((own, columns) + tile, jnp.float32),
+            pltpu.VMEM((components, own, columns) + tile, jnp.float32),
+            pltpu.VMEM((components, own, columns) + tile, jnp.float32),
+            pltpu.VMEM((outer, components, planes, own, LANES), jnp.float32),
+            pltpu.VMEM(ahead.shape, jnp.bfloat16),
+            pltpu.VMEM(pairs.shape, jnp.bfloat16),
+            pltpu.VMEM(back.shape, jnp.bfloat16),
+            pltpu.SemaphoreType.DMA((3,)),
+            pltpu.SemaphoreType.DMA((kinds,)),
+            pltpu.SemaphoreType.DMA((kinds,)),
+        ],
+        compiler_params=pltpu.CompilerParams(collective_id=0, has_side_effects=True),
+    )(
+        template.reshape((extent_x,) + tile),
+        target.reshape((extent_x,) + tile),
+        velocity.reshape((components, extent_x) + tile),
+        departure.reshape(departure.shape[:2] + tile),
+        weights,
+        jnp.asarray(ahead),
+        jnp.asarray(pairs),
+        jnp.asarray(back),
+    )
+    return result.reshape(components, planes, own, outer * LANES)
+
+
+def per_block(template, target, velocity, departure, weights):
+    rows, columns = lax.axis_size("row"), lax.axis_size("col")
+    one_line = template.shape[1] == 1 and rows % columns == 0 and rows > 2
+    whole_tiles = template.shape[2] % (LANES * SUBLANES) == 0
+    short = rows // columns % SUBLANES == 0 and rows >= 8
+    if one_line and whole_tiles and short:
+        return direct(template, target, velocity, departure, weights)
+    return per_device(template, target, velocity, departure, weights)
+
+
 def solution(mesh):
     in_specs = (
         P(None, "row", "col"),
@@ -155,5 +605,5 @@
     )
     out_specs = P(None, "row", "col", None)
     return jax.shard_map(
-        per_device, mesh=mesh, in_specs=in_specs, out_specs=out_specs, check_vma=False
-    )
+        per_block, mesh=mesh, in_specs=in_specs, out_specs=out_specs, check_vma=False
+    )

time: 1360 us -> 38 us (0.03)
  local copies, waits for them, and re-layouts: 1290 us -> 3.15 us
  waiting for transfers between devices: 42.4 us -> 0 us
  Pallas kernels: 0 us -> 34.5 us
  starting transfers between devices: 15.6 us -> 0 us
    gather x8 -> x0, local copies, waits for them, and re-layouts: 1280 us -> none  [transport(): jnp.take_along_axis(template_y, source_index, axis=1)]
    all_to_all x2 -> x0, waiting for transfers between devices: 37.3 us -> none  [the longest x1 21.4 us: per_device(): lax.all_to_all(bundle, 'row', split_axis=1, concat_axis=2, tiled=True)]
    pallas_call x0 -> x1, Pallas kernels: none -> 34.5 us  [direct(): pl.pallas_call(functools.partial(kernel, (rows, columns)), out_shape=jax....]
  transfers between devices with their start and end apart: 4 -> 0, of which waited for: 4 -> 0; matrix products, arithmetic and copies ran while one was open for 0% -> 0% of each run, Pallas kernels for 0% -> 0%
where the time goes in v1:
time: 38 us; the launch traced here: 37.7 us
  Pallas kernels  34.5 us (91%)
  local copies, waits for them, and re-layouts  3.15 us (8%)
    pallas_call x1, Pallas kernels, direct(): pl.pallas_call(functools.partial(kernel, (rows, columns)), out_shape=jax....  34.5 us
    reshape x1, local copies, waits for them, and re-layouts, direct(): return result.reshape(components, planes, own, outer * LANES)  1.81 us
    unnamed x1, local copies, waits for them, and re-layouts  1.35 us

profile of v1, /device:TPU:0, one launch (start us, length us, event | category | flops | bytes accessed | tf_op | source)
XLA Modules:
  0.0 37.7 jit_solution(17820905998697573152)
XLA Ops:
  0.0 1.3 %copy.9.weights = f32[8,4]{1,0:T(8,128)} copy(f32[8,4]{0,1:T(4,128)} %param.12) | data formatting | bytes 256 | tf_op args[4]
  1.3 34.5 %shard_map.82 = f32[3,2,8,16,128]{4,3,2,1,0:T(8,128)} custom-call(f32[32,8,128]{2,1,0:T(8,128)} %bitcast.7, f32[32,8,128]{2,1,0:T(8,128)} %bitcast.8, f32[3,32,8,128]{3,2,1,0:T(8,128)} %bitcast.6, s32[2,1,8,128]{3,2,1,0:T(8,128)} %bitcast.9, f32[8,4]{1,0:T(8,128)} %copy.9.weights, bf16[2,128,128]{2,1,0:T(8,128)(2,1)} %constant.6.clone.ahead_hbm, ...), custom_call_target="tpu_custom_call" | custom-call | tf_op jit(solution)/shard_map/pallas_call | solution.py:551
  35.9 1.8 %reshape.19 = f32[3,2,8,2048]{3,2,1,0:T(8,128)} reshape(f32[3,2,8,16,128]{4,3,2,1,0:T(8,128)} %shard_map.82) | data formatting | bytes 786432 | tf_op jit(solution)/shard_map/reshape | solution.py:585

commit v2 on v1

--- a/solution.py
+++ b/solution.py
@@ -209,7 +209,9 @@
         inverse[:, 2 * k + 1] = -2.0 * np.sin(phase) / outer
     same = np.eye(rows)
     ahead = np.einsum("ka,yz->kyza", forward, same).reshape(outer * rows, rows * outer)
-    back = np.einsum("ak,yz->yakz", inverse, same).reshape(rows * outer, outer * rows)
+    back = np.einsum("ak,yz->aykz", inverse, same).reshape(outer * rows, outer * rows)
+    moves = np.einsum("ab,yz->ayzb", np.eye(outer), same).reshape(outer * rows, rows * outer)
+    back = np.concatenate([back, moves], axis=1)
     return halves_of(ahead), halves_of(np.stack(pairs)), halves_of(back)
 
 
@@ -227,12 +229,12 @@
     template_y,
     target_z,
     velocity_z,
+    edge,
     extended,
     moved,
     moved_low,
     moved_high,
-    velocity_low,
-    velocity_high,
+    rest,
     spectrum,
     ahead,
     pairs,
@@ -250,7 +252,10 @@
     owner = row // own
     place = lax.rem(row, own)
     TEMPLATE, TARGET, MOVED, LOW, HIGH_SIDE, VELOCITY = 0, 1, 2, 3, 4, 5
-    VLOW, VHIGH = VELOCITY + components, VELOCITY + 2 * components
+    SIDE, EDGE = VELOCITY + components, VELOCITY + 2 * components
+    extent_x = velocity.shape[1]
+    parity = lax.rem(row, 2)
+    groups = [pl.ds(0, 1), pl.ds(1, components - 1)]
 
     loads = [
         pltpu.make_async_copy(source, sink, load_sem.at[i])
@@ -307,7 +312,7 @@
     def arrived(ref, kind):
         pltpu.make_async_copy(ref, ref, recv_sem.at[kind]).wait()
 
-    order = list(range(1, rows)) + [0]
+    order = sorted(range(rows), key=lambda i: abs(2 * i - rows))
     for i, to in exchange(order):
         source = template.at[pl.ds(to * planes, planes)]
         sink = template_y.at[:, row]
@@ -326,65 +331,78 @@
     before = lax.rem(owner + columns - 1, columns)
     after = lax.rem(owner + 1, columns)
 
-    def send_velocity(comp):
+    def act(copy, where, start):
+        @pl.when(where == column)
+        def _():
+            if start:
+                pltpu.make_async_copy(copy[0], copy[1], recv_sem.at[copy[2]]).start()
+
+        @pl.when(where != column)
+        def _():
+            if start:
+                remote(*copy).start()
+            else:
+                remote(*copy).wait_send()
+
+    def act_any(copy, where, i, start):
+        if i == 0:
+            act(copy, where, start)
+        elif start:
+            remote(*copy).start()
+        else:
+            remote(*copy).wait_send()
+
+    def velocity_copies(group, start):
+        comps = groups[group]
         for i, to in exchange(order):
-            source = velocity.at[comp, pl.ds(to * planes, planes)]
-            deliver(
-                source,
-                velocity_z.at[comp, :, place + 1, column],
-                VELOCITY + comp,
-                (to, owner),
-                owner if i == 0 else None,
-            )
-
-    def edges(act):
+            odd = lax.rem(to, 2)
+            first = to * planes - 1 + odd
+
+            def piece(low, count, at):
+                copy = (
+                    velocity.at[comps, pl.ds(low, count)],
+                    velocity_z.at[comps, pl.ds(at, count), place, column],
+                    VELOCITY + group,
+                    (to, owner),
+                )
+                act_any(copy, owner, i, start)
+
+            @pl.when(jnp.logical_and(to > 0, to < rows - 1))
+            def _():
+                piece(first, planes + 1, odd)
+
+            @pl.when(to == 0)
+            def _():
+                piece(0, planes, 1)
+                piece(extent_x - 1, 1, 0)
+
+            @pl.when(to == rows - 1)
+            def _():
+                piece(extent_x - planes, planes, 1)
+                piece(0, 1, planes + 1)
+
+    def edge_copies(group, start):
+        comps = groups[group]
+
+        def send(line, where):
+            for i, to in exchange(order):
+                copy = (
+                    velocity.at[comps, pl.ds(to * planes, planes)],
+                    edge.at[comps, :, line, column],
+                    EDGE + group,
+                    (to, where),
+                )
+                act_any(copy, where, i, start)
+
         @pl.when(place == 0)
         def _():
-            for comp in range(components):
-                for i, to in exchange(order):
-                    act(comp, i, to, own + 1, before)
+            send(1, before)
 
         @pl.when(place == own - 1)
         def _():
-            for comp in range(components):
-                for i, to in exchange(order):
-                    act(comp, i, to, 0, after)
-
-    def edge_copy(comp, to, line, where):
-        return (
-            velocity.at[comp, pl.ds(to * planes, planes)],
-            velocity_z.at[comp, :, line, column],
-            VELOCITY + comp,
-            (to, where),
-        )
-
-    def start_edge(comp, i, to, line, where):
-        copy = edge_copy(comp, to, line, where)
-        if i > 0:
-            remote(*copy).start()
-            return
-
-        @pl.when(where == column)
-        def _():
-            pltpu.make_async_copy(copy[0], copy[1], recv_sem.at[copy[2]]).start()
-
-        @pl.when(where != column)
-        def _():
-            remote(*copy).start()
-
-    def wait_edge(comp, i, to, line, where):
-        copy = edge_copy(comp, to, line, where)
-        if i > 0:
-            remote(*copy).wait_send()
-            return
-
-        @pl.when(where != column)
-        def _():
-            remote(*copy).wait_send()
-
-    edges(start_edge)
-    for comp in range(components):
-        send_velocity(comp)
+            send(0, after)
+
+    velocity_copies(0, True)
 
     arrived(template_y, TEMPLATE)
     blocks = departure.shape[1]
@@ -395,7 +413,7 @@
             offset = departure[plane, block]
             whole = offset >> (QUANT.bit_length() - 1)
             levels = offset - whole * QUANT
-            taps = tap_weights(levels, lambda level, tap: weights[level, tap])
+            taps = tap_weights(levels, lambda level, tap: weights[tap, level])
             shift = jnp.where(whole + 1 < 0, whole + 1 + lines, whole + 1)
             rolled = image
             step = 1
@@ -431,6 +449,9 @@
             extended.at[planes - 1, lines_of], moved_low.at[:, column], LOW, (up, to), None
         )
         deliver(extended.at[0, lines_of], moved_high.at[:, column], HIGH_SIDE, (down, to), None)
+    edge_copies(0, True)
+    edge_copies(1, True)
+    velocity_copies(1, True)
     moved[column] = extended[:, pl.ds(column * own, own + 2)]
     for load in loads:
         load.wait()
@@ -440,29 +461,7 @@
 
     ahead_parts = (ahead[0], ahead[1])
     back_parts = (back[0], back[1])
-    for comp in range(components):
-        arrived(velocity_z.at[comp], VELOCITY + comp)
-        deliver(
-            velocity_z.at[comp, planes - 1, pl.ds(1, own)],
-            velocity_low.at[comp],
-            VLOW + comp,
-            (up, column),
-            None,
-        )
-        deliver(
-            velocity_z.at[comp, 0, pl.ds(1, own)],
-            velocity_high.at[comp],
-            VHIGH + comp,
-            (down, column),
-            None,
-        )
-        for plane in range(planes):
-            block = velocity_z[comp, plane, 1 : own + 1].reshape(own * outer, LANES)
-            spectrum[:, comp, plane] = dot_split(ahead_parts, split_halves(block)).reshape(
-                outer, own, LANES
-            )
-        if comp > 0:
-            continue
+    def force():
         arrived(target_z, TARGET)
         for _ in range(columns - 1):
             pltpu.make_async_copy(moved.at[0], moved.at[0], recv_sem.at[MOVED]).wait()
@@ -486,13 +485,32 @@
                     [moved[j, index, 1 : own + 1] for j in range(columns)], axis=1
                 )
 
-            out[0, plane] = half * (at(plane + 1) - at(plane - 1))
-            out[1, plane] = half * (with_ends[2:] - with_ends[:-2])
+            rest[0, plane] = half * (at(plane + 1) - at(plane - 1))
+            rest[1, plane] = half * (with_ends[2:] - with_ends[:-2])
             following = jnp.roll(here, -1, 2)
             following = jnp.where(lane == LANES - 1, jnp.roll(following, -1, 1), following)
             previous = jnp.roll(here, 1, 2)
             previous = jnp.where(lane == 0, jnp.roll(previous, 1, 1), previous)
-            out[2, plane] = half * (following - previous)
+            rest[2, plane] = half * (following - previous)
+
+    for group, comps in enumerate(groups):
+        if group == len(groups) - 1:
+            force()
+        arrived(velocity_z.at[comps, pl.ds(parity, planes + 1)], VELOCITY + group)
+        arrived(edge.at[comps], EDGE + group)
+        deliver(
+            velocity_z.at[comps, planes - (planes - 1) * parity],
+            velocity_z.at[comps, (planes + 1) * parity],
+            SIDE + group,
+            (row + 1 - 2 * parity, column),
+            None,
+        )
+        for comp in range(comps.start, comps.start + comps.size):
+            for plane in range(planes):
+                block = velocity_z[comp, plane + 1].reshape(own * outer, LANES)
+                spectrum[:, comp, plane] = dot_split(ahead_parts, split_halves(block)).reshape(
+                    outer, own, LANES
+                )
 
     for pair in range(outer // 2):
         shape = (components * planes * own, LANES)
@@ -505,21 +523,29 @@
         spectrum[2 * pair + 1] = result[:, LANES:].reshape(shape)
 
     for comp in range(components):
-        arrived(velocity_low.at[comp], VLOW + comp)
-        arrived(velocity_high.at[comp], VHIGH + comp)
+        for group, comps in enumerate(groups):
+            if comps.start == comp:
+                arrived(velocity_z.at[comps, (planes + 1) * (1 - parity)], SIDE + group)
         for plane in range(planes):
-            block = spectrum[:, comp, plane].reshape(outer * own, LANES)
-            smooth = dot_split(back_parts, split_halves(block)).reshape(own, outer, LANES)
-            low = velocity_low[comp] if plane == 0 else velocity_z[comp, plane - 1, 1 : own + 1]
-            high = (
-                velocity_high[comp]
-                if plane == planes - 1
-                else velocity_z[comp, plane + 1, 1 : own + 1]
+            lined = jnp.concatenate(
+                [edge[comp, plane, 0:1], velocity_z[comp, plane + 1], edge[comp, plane, 1:2]], axis=0
             )
-            sides = whole_lines(
-                (low + high) + (velocity_z[comp, plane, :own] + velocity_z[comp, plane, 2:])
+            sides = (velocity_z[comp, plane] + velocity_z[comp, plane + 2]) + (
+                lined[:own] + lined[2:]
             )
-            out[comp, plane] = out[comp, plane] + (smooth - BETA * sides)
+            other = rest[comp, plane] - BETA * whole_lines(sides)
+            block = jnp.concatenate(
+                [
+                    spectrum[:, comp, plane].reshape(outer * own, LANES),
+                    other.reshape(own * outer, LANES),
+                ],
+                axis=0,
+            )
+            result = dot_split(back_parts, split_halves(block))
+            for group in range(outer):
+                out[comp, plane, :, group * LANES : (group + 1) * LANES] = result[
+                    group * own : (group + 1) * own
+                ]
 
     for near, source, sink, kind, to in pending:
         if near is None:
@@ -530,7 +556,9 @@
             def _():
                 remote(source, sink, kind, to).wait_send()
 
-    edges(wait_edge)
+    for group in range(len(groups)):
+        velocity_copies(group, False)
+        edge_copies(group, False)
 
 
 def direct(template, target, velocity, departure, weights):
@@ -548,21 +576,21 @@
     vmem = pl.BlockSpec(memory_space=pltpu.VMEM)
     smem = pl.BlockSpec(memory_space=pltpu.SMEM)
     kinds = 5 + 3 * components
-    result = pl.pallas_call(
+    return pl.pallas_call(
         functools.partial(kernel, (rows, columns)),
-        out_shape=jax.ShapeDtypeStruct((components, planes, own, outer, LANES), jnp.float32),
+        out_shape=jax.ShapeDtypeStruct((components, planes, own, outer * LANES), jnp.float32),
         in_specs=[hbm, hbm, hbm, vmem, smem, hbm, hbm, hbm],
         out_specs=vmem,
         scratch_shapes=[
             pltpu.VMEM((planes, lines) + tile, jnp.float32),
             pltpu.VMEM((planes, own, columns) + tile, jnp.float32),
-            pltpu.VMEM((components, planes, own + 2, columns) + tile, jnp.float32),
+            pltpu.VMEM((components, planes + 2, own, columns) + tile, jnp.float32),
+            pltpu.VMEM((components, planes, 2, columns) + tile, jnp.float32),
             pltpu.VMEM((planes, lines + 2) + tile, jnp.float32),
             pltpu.VMEM((columns, planes, own + 2) + tile, jnp.float32),
             pltpu.VMEM((own, columns) + tile, jnp.float32),
             pltpu.VMEM((own, columns) + tile, jnp.float32),
-            pltpu.VMEM((components, own, columns) + tile, jnp.float32),
-            pltpu.VMEM((components, own, columns) + tile, jnp.float32),
+            pltpu.VMEM((components, planes, own, outer, LANES), jnp.float32),
             pltpu.VMEM((outer, components, planes, own, LANES), jnp.float32),
             pltpu.VMEM(ahead.shape, jnp.bfloat16),
             pltpu.VMEM(pairs.shape, jnp.bfloat16),
@@ -577,17 +605,16 @@
         target.reshape((extent_x,) + tile),
         velocity.reshape((components, extent_x) + tile),
         departure.reshape(departure.shape[:2] + tile),
-        weights,
+        weights.T,
         jnp.asarray(ahead),
         jnp.asarray(pairs),
         jnp.asarray(back),
     )
-    return result.reshape(components, planes, own, outer * LANES)
 
 
 def per_block(template, target, velocity, departure, weights):
     rows, columns = lax.axis_size("row"), lax.axis_size("col")
-    one_line = template.shape[1] == 1 and rows % columns == 0 and rows > 2
+    one_line = template.shape[1] == 1 and rows % columns == 0 and rows % 2 == 0 and rows > 2
     whole_tiles = template.shape[2] % (LANES * SUBLANES) == 0
     short = rows // columns % SUBLANES == 0 and rows >= 8
     if one_line and whole_tiles and short:

time: 38 us -> 33.6 us (0.88)
  the two profiles are of different devices: /device:TPU:0 before, /device:TPU:17 now
where the time goes in v2:
time: 33.6 us; the launch traced here: 33.4 us
  Pallas kernels  31.6 us (94%)
  local copies, waits for them, and re-layouts  1.77 us (5%)
    pallas_call x1, Pallas kernels, direct(): pl.pallas_call(functools.partial(kernel, (rows, columns)), out_shape=jax....  31.6 us
    unnamed x1, local copies, waits for them, and re-layouts  1.77 us

profile of v2, /device:TPU:17, one launch (start us, length us, event | category | flops | bytes accessed | tf_op | source)
XLA Modules:
  0.0 33.4 jit_solution(17116347668244141937)
XLA Ops:
  0.0 31.6 %shard_map.82 = f32[3,2,8,2048]{3,2,1,0:T(8,128)} custom-call(f32[32,8,128]{2,1,0:T(8,128)} %bitcast.6, f32[32,8,128]{2,1,0:T(8,128)} %bitcast.7, f32[3,32,8,128]{3,2,1,0:T(8,128)} %bitcast.5, s32[2,1,8,128]{3,2,1,0:T(8,128)} %bitcast.8, f32[4,8]{1,0:T(4,128)} %bitcast.9, bf16[2,128,128]{2,1,0:T(8,128)(2,1)} %constant.6.clone.ahead_hbm, ...), custom_call_target="tpu_custom_call" | custom-call | tf_op jit(solution)/shard_map/pallas_call | solution.py:579
  31.6 1.8 %copy.10 = f32[3,2,8,2048]{3,2,1,0:T(8,128)} copy(f32[3,2,8,2048]{3,2,1,0:T(8,128)} %shard_map.82) | data formatting | bytes 786432

commit v3 on v2

--- a/solution.py
+++ b/solution.py
@@ -160,6 +160,9 @@
     slope_across = (padded[2:] - padded[:-2]) * 0.5
     force = jnp.stack([misfit_z * slope_across, columns_z[2], misfit_z * central(moved_z, 2)])
     return BETA * (second_z + bending) + force
+
+
+QUAD = 4
 
 
 def split_halves(values):
@@ -252,10 +255,10 @@
     owner = row // own
     place = lax.rem(row, own)
     TEMPLATE, TARGET, MOVED, LOW, HIGH_SIDE, VELOCITY = 0, 1, 2, 3, 4, 5
-    SIDE, EDGE = VELOCITY + components, VELOCITY + 2 * components
+    SIDE_LOW, SIDE_HIGH, EDGE_LOW, EDGE_HIGH = (VELOCITY + i * components for i in range(1, 5))
     extent_x = velocity.shape[1]
-    parity = lax.rem(row, 2)
-    groups = [pl.ds(0, 1), pl.ds(1, components - 1)]
+    spot = lax.rem(row, QUAD)
+    groups = [pl.ds(0, components - 1), pl.ds(components - 1, 1)]
 
     loads = [
         pltpu.make_async_copy(source, sink, load_sem.at[i])
@@ -331,76 +334,102 @@
     before = lax.rem(owner + columns - 1, columns)
     after = lax.rem(owner + 1, columns)
 
-    def act(copy, where, start):
-        @pl.when(where == column)
-        def _():
+    def away_start(*copy):
+        remote(*copy).start()
+
+    def away_wait(*copy):
+        remote(*copy).wait_send()
+
+    def inside(source, sink, kind, _):
+        pltpu.make_async_copy(source, sink, recv_sem.at[kind]).start()
+
+    def velocity_copies(group, start):
+        comps = groups[group]
+        for i, to in exchange(order):
+            at_spot = lax.rem(to, QUAD)
+            first = to * planes
+            case = jnp.where(at_spot == 0, 0, jnp.where(at_spot == QUAD - 1, 2, 1))
+            case = jnp.where(to == 0, 3, jnp.where(to == rows - 1, 4, case))
+
+            def pieces(case, act):
+                def piece(low, count, at):
+                    act(
+                        velocity.at[comps, pl.ds(low, count)],
+                        velocity_z.at[comps, pl.ds(at, count), place, column],
+                        VELOCITY + group,
+                        (to, owner),
+                    )
+
+                @pl.when(case == 1)
+                def _():
+                    piece(first, planes, 1)
+
+                @pl.when(case == 0)
+                def _():
+                    piece(first - 1, planes + 1, 0)
+
+                @pl.when(case == 2)
+                def _():
+                    piece(first, planes + 1, 1)
+
+                @pl.when(case == 3)
+                def _():
+                    piece(0, planes, 1)
+                    piece(extent_x - 1, 1, 0)
+
+                @pl.when(case == 4)
+                def _():
+                    piece(extent_x - planes, planes, 1)
+                    piece(0, 1, planes + 1)
+
+            away = away_start if start else away_wait
+            if i > 0:
+                pieces(case, away)
+                continue
+            pieces(jnp.where(owner == column, -1, case), away)
             if start:
-                pltpu.make_async_copy(copy[0], copy[1], recv_sem.at[copy[2]]).start()
-
-        @pl.when(where != column)
-        def _():
+                pieces(jnp.where(owner == column, case, -1), inside)
+
+    def beside(group, start):
+        comps = groups[group]
+        mine = pl.ds(1, planes)
+
+        def go(*copy):
             if start:
                 remote(*copy).start()
             else:
                 remote(*copy).wait_send()
 
-    def act_any(copy, where, i, start):
-        if i == 0:
-            act(copy, where, start)
-        elif start:
-            remote(*copy).start()
-        else:
-            remote(*copy).wait_send()
-
-    def velocity_copies(group, start):
-        comps = groups[group]
-        for i, to in exchange(order):
-            odd = lax.rem(to, 2)
-            first = to * planes - 1 + odd
-
-            def piece(low, count, at):
-                copy = (
-                    velocity.at[comps, pl.ds(low, count)],
-                    velocity_z.at[comps, pl.ds(at, count), place, column],
-                    VELOCITY + group,
-                    (to, owner),
-                )
-                act_any(copy, owner, i, start)
-
-            @pl.when(jnp.logical_and(to > 0, to < rows - 1))
-            def _():
-                piece(first, planes + 1, odd)
-
-            @pl.when(to == 0)
-            def _():
-                piece(0, planes, 1)
-                piece(extent_x - 1, 1, 0)
-
-            @pl.when(to == rows - 1)
-            def _():
-                piece(extent_x - planes, planes, 1)
-                piece(0, 1, planes + 1)
-
-    def edge_copies(group, start):
-        comps = groups[group]
-
-        def send(line, where):
-            for i, to in exchange(order):
-                copy = (
-                    velocity.at[comps, pl.ds(to * planes, planes)],
-                    edge.at[comps, :, line, column],
-                    EDGE + group,
-                    (to, where),
-                )
-                act_any(copy, where, i, start)
-
-        @pl.when(place == 0)
+        go(
+            velocity_z.at[comps, mine, own - 1],
+            edge.at[comps, :, 0],
+            EDGE_LOW + group,
+            (row, lax.rem(column + 1, columns)),
+        )
+        go(
+            velocity_z.at[comps, mine, 0],
+            edge.at[comps, :, 1],
+            EDGE_HIGH + group,
+            (row, lax.rem(column + columns - 1, columns)),
+        )
+
+        @pl.when(spot < QUAD - 1)
         def _():
-            send(1, before)
-
-        @pl.when(place == own - 1)
+            go(
+                velocity_z.at[comps, planes],
+                velocity_z.at[comps, 0],
+                SIDE_LOW + group,
+                (lax.rem(row + 1, rows), column),
+            )
+
+        @pl.when(spot > 0)
         def _():
-            send(0, after)
+            go(
+                velocity_z.at[comps, 1],
+                velocity_z.at[comps, planes + 1],
+                SIDE_HIGH + group,
+                (lax.rem(row + rows - 1, rows), column),
+            )
 
     velocity_copies(0, True)
 
@@ -449,8 +478,6 @@
             extended.at[planes - 1, lines_of], moved_low.at[:, column], LOW, (up, to), None
         )
         deliver(extended.at[0, lines_of], moved_high.at[:, column], HIGH_SIDE, (down, to), None)
-    edge_copies(0, True)
-    edge_copies(1, True)
     velocity_copies(1, True)
     moved[column] = extended[:, pl.ds(column * own, own + 2)]
     for load in loads:
@@ -496,15 +523,20 @@
     for group, comps in enumerate(groups):
         if group == len(groups) - 1:
             force()
-        arrived(velocity_z.at[comps, pl.ds(parity, planes + 1)], VELOCITY + group)
-        arrived(edge.at[comps], EDGE + group)
-        deliver(
-            velocity_z.at[comps, planes - (planes - 1) * parity],
-            velocity_z.at[comps, (planes + 1) * parity],
-            SIDE + group,
-            (row + 1 - 2 * parity, column),
-            None,
-        )
+
+        @pl.when(spot == 0)
+        def _():
+            arrived(velocity_z.at[comps, pl.ds(0, planes + 1)], VELOCITY + group)
+
+        @pl.when(spot == QUAD - 1)
+        def _():
+            arrived(velocity_z.at[comps, pl.ds(1, planes + 1)], VELOCITY + group)
+
+        @pl.when(spot * (QUAD - 1 - spot) > 0)
+        def _():
+            arrived(velocity_z.at[comps, pl.ds(1, planes)], VELOCITY + group)
+
+        beside(group, True)
         for comp in range(comps.start, comps.start + comps.size):
             for plane in range(planes):
                 block = velocity_z[comp, plane + 1].reshape(own * outer, LANES)
@@ -525,7 +557,17 @@
     for comp in range(components):
         for group, comps in enumerate(groups):
             if comps.start == comp:
-                arrived(velocity_z.at[comps, (planes + 1) * (1 - parity)], SIDE + group)
+                arrived(edge.at[comps, :, 0], EDGE_LOW + group)
+                arrived(edge.at[comps, :, 1], EDGE_HIGH + group)
+
+                @pl.when(spot > 0)
+                def _():
+                    arrived(velocity_z.at[comps, 0], SIDE_LOW + group)
+
+                @pl.when(spot < QUAD - 1)
+                def _():
+                    arrived(velocity_z.at[comps, planes + 1], SIDE_HIGH + group)
+
         for plane in range(planes):
             lined = jnp.concatenate(
                 [edge[comp, plane, 0:1], velocity_z[comp, plane + 1], edge[comp, plane, 1:2]], axis=0
@@ -558,7 +600,7 @@
 
     for group in range(len(groups)):
         velocity_copies(group, False)
-        edge_copies(group, False)
+        beside(group, False)
 
 
 def direct(template, target, velocity, departure, weights):
@@ -575,10 +617,10 @@
     hbm = pl.BlockSpec(memory_space=pl.ANY)
     vmem = pl.BlockSpec(memory_space=pltpu.VMEM)
     smem = pl.BlockSpec(memory_space=pltpu.SMEM)
-    kinds = 5 + 3 * components
+    kinds = 5 + 5 * components
     return pl.pallas_call(
         functools.partial(kernel, (rows, columns)),
-        out_shape=jax.ShapeDtypeStruct((components, planes, own, outer * LANES), jnp.float32),
+        out_shape=pltpu.VMEM((components, planes, own, outer * LANES), jnp.float32),
         in_specs=[hbm, hbm, hbm, vmem, smem, hbm, hbm, hbm],
         out_specs=vmem,
         scratch_shapes=[
@@ -614,7 +656,8 @@
 
 def per_block(template, target, velocity, departure, weights):
     rows, columns = lax.axis_size("row"), lax.axis_size("col")
-    one_line = template.shape[1] == 1 and rows % columns == 0 and rows % 2 == 0 and rows > 2
+    components = velocity.shape[0]
+    one_line = template.shape[1] == 1 and rows % columns == 0 and rows % QUAD == 0 and columns > 1 and components > 1
     whole_tiles = template.shape[2] % (LANES * SUBLANES) == 0
     short = rows // columns % SUBLANES == 0 and rows >= 8
     if one_line and whole_tiles and short:

time: 33.6 us -> 31.2 us (0.929)
  the two profiles are of different devices: /device:TPU:17 before, /device:TPU:0 now
where the time goes in v3:
time: 31.2 us; the launch traced here: 31 us
  Pallas kernels  30.2 us (97%)
  local copies, waits for them, and re-layouts  0.75 us (2%)
    pallas_call x1, Pallas kernels, direct(): pl.pallas_call(functools.partial(kernel, (rows, columns)), out_shape=pltp...  30.2 us
    unnamed x1, local copies, waits for them, and re-layouts  0.75 us

profile of v3, /device:TPU:0, one launch (start us, length us, event | category | flops | bytes accessed | tf_op | source)
XLA Modules:
  0.0 31.0 jit_solution(16753624450263709606)
XLA Ops:
  0.0 30.2 %shard_map.82 = f32[3,2,8,2048]{3,2,1,0:T(8,128)S(1)} custom-call(f32[32,8,128]{2,1,0:T(8,128)} %bitcast.6, f32[32,8,128]{2,1,0:T(8,128)} %bitcast.7, f32[3,32,8,128]{3,2,1,0:T(8,128)} %bitcast.5, s32[2,1,8,128]{3,2,1,0:T(8,128)} %bitcast.8, f32[4,8]{1,0:T(4,128)} %bitcast.9, bf16[2,128,128]{2,1,0:T(8,128)(2,1)} %constant.6.clone.ahead_hbm, ...), custom_call_target="tpu_custom_call" | custom-call | tf_op jit(solution)/shard_map/pallas_call | solution.py:621
  30.2 0.7 %copy.10 = f32[3,2,8,2048]{3,2,1,0:T(8,128)} copy(f32[3,2,8,2048]{3,2,1,0:T(8,128)S(1)} %shard_map.82) | data formatting | bytes 786432
